TPU v7x, 256 devices: a whole 4x4x8 slice. The times are simulated.
256 devices in a mesh: row: 16 (over x, y), col: 16 (over z, core).
Axes of the slice: x: 4, y: 4, z: 8, core: 2. Of those that a mesh axis runs over, the one named last changes fastest.
Arguments:
- target: float32 [8, 16, 128, 8, 16, 128], P(None, 'row', None, None, 'col'), may hold values from -6 to 6
- panel_a: bfloat16 [2, 32, 128, 512], P(None, 'col'), may hold values from -1.1953125 to 1.1953125
- inv_factor: bfloat16 [2, 512, 512], replicated, as said below
- panel_rhs: bfloat16 [2, 512, 256], P(None, 'col'), may hold values from -6 to 6
- panel_rows: int32 [2, 32], replicated, may hold values from 0 to 127, as said below
- right_sides: float32 [8, 16, 128, 256], P(None, 'col'), may hold values from -12 to 12
Outputs:
- updated_target: float32 [8, 16, 128, 8, 16, 128], P(None, 'row', None, None, 'col')
- updated_sides: float32 [8, 16, 128, 256], P(None, 'col')
Inputs may be any that keep to these rules, and one draw needn't show every extreme that they name: `panel_rows`: each row holds 32 distinct positions in increasing order, the first 0 and the last 127. `inv_factor`: lower triangular, diagonal between 0.5 and 2.
All inputs are finite; a program needn't handle non-finite values.
Results may differ from a plain program's by a relative error of at most 0.0035.
Values may be sent and summed in bfloat16 or wider, within the bound.
A program may use at most 128 MiB of HBM per device.

v0:
```python
import jax
import jax.numpy as jnp
from jax import lax
from jax.sharding import PartitionSpec as P


def shards(target, panel_a, inv_factor, panel_rhs, panel_rows, right_sides):
    row_count = lax.axis_size("row")
    col_count = lax.axis_size("col")
    row_index = lax.axis_index("row")
    col_index = lax.axis_index("col")
    tile_rows = target.shape[2]
    row_blocks = target.shape[0]
    col_blocks = target.shape[3]
    slab_rows = tile_rows // row_count
    shard_rows = panel_rhs.shape[1]
    updated_target = target
    updated_sides = right_sides
    row_places = jnp.arange(row_blocks, dtype=jnp.int32) * row_count + row_index
    col_places = jnp.arange(col_blocks, dtype=jnp.int32) * col_count + col_index
    for which_panel in range(2):
        factor = inv_factor[which_panel]
        positions = panel_rows[which_panel]
        own_rows = lax.dynamic_slice_in_dim(
            panel_a[which_panel], row_index * slab_rows, slab_rows, 1
        )
        solved_piece = jnp.einsum(
            "axq,pq->axp", own_rows, factor, preferred_element_type=jnp.float32
        ).astype(jnp.bfloat16)
        column_tiles = lax.all_gather(solved_piece, "row", axis=1, tiled=True)
        all_tiles = lax.all_gather(column_tiles, "col", axis=0, tiled=True)
        columns = lax.dynamic_slice_in_dim(factor, col_index * shard_rows, shard_rows, 1)
        local_term = jnp.dot(columns, panel_rhs[which_panel], preferred_element_type=jnp.float32)
        partial_value = lax.psum(local_term, "col").astype(jnp.bfloat16)
        pick_rows = (positions[None, :] == row_places[:, None]).astype(jnp.bfloat16)
        pick_cols = (positions[None, :] == col_places[:, None]).astype(jnp.bfloat16)
        row_set = jnp.einsum(
            "ia,axp->ixp", pick_rows, all_tiles, preferred_element_type=jnp.float32
        ).astype(jnp.bfloat16)
        col_set = jnp.einsum(
            "ka,axp->kxp", pick_cols, all_tiles, preferred_element_type=jnp.float32
        ).astype(jnp.bfloat16)
        schur_term = jnp.einsum(
            "ixp,kyp->ixky", row_set, col_set, preferred_element_type=jnp.float32
        )
        updated_target = updated_target - schur_term[:, None, :, :, None, :]
        side_term = jnp.einsum(
            "kxp,pn->kxn", col_set, partial_value, preferred_element_type=jnp.float32
        )
        updated_sides = updated_sides - side_term[:, None]
    return (updated_target, updated_sides)


def solution(mesh):
    placed = (
        P(None, "row", None, None, "col", None),
        P(None, "col", None, None),
        P(),
        P(None, "col", None),
        P(),
        P(None, "col", None, None),
    )
    return jax.shard_map(
        shards,
        mesh=mesh,
        in_specs=placed,
        out_specs=(P(None, "row", None, None, "col", None), P(None, "col", None, None)),
        check_vma=False,
    )
```

profile of v0, /device:TPU:0, one launch (start us, length us, event | category | flops | bytes accessed | tf_op | source)
XLA Modules:
  0.0 168.0 jit_solution(11555292527745360764)
XLA Ops:
  7.2 0.0 all-gather.5.cloned.1.call-start
  7.2 1.1 fusion.73
  8.3 1.3 convolution_convert_fusion
  9.6 24.2 %all_gather.14 = bf16[2,128,512]{2,1,0:T(8,128)(2,1)} all-gather(bf16[2,8,512]{2,1,0:T(8,128)(2,1)S(1)} %convolution_convert_fusion), channel_id=1, replica_groups=mesh['row'=16,'col'=16] {'row'}, dimensions={1}, use_global_device_ids=true | all-gather | bytes 278528 | tf_op jit(solution)/shard_map/all_gather | solution.py:30
  33.8 0.0 all-gather.5.cloned.1.call-update
  33.8 0.0 all-gather.3.cloned.1.call-start
  33.9 1.3 convolution_convert_fusion.1
  35.2 25.0 %all_gather.12 = bf16[2,128,512]{2,1,0:T(8,128)(2,1)} all-gather(bf16[2,8,512]{2,1,0:T(8,128)(2,1)S(1)} %convolution_convert_fusion.1), channel_id=1, replica_groups=mesh['row'=16,'col'=16] {'row'}, dimensions={1}, use_global_device_ids=true | all-gather | bytes 278528 | tf_op jit(solution)/shard_map/all_gather | solution.py:30
  60.2 0.0 all-gather.3.cloned.1.call-update
  60.2 1.3 fusion.72
  61.5 0.3 fusion.34
  61.8 0.3 fusion.36
  62.1 69.4 %all-reduce.2 = (bf16[512,256]{1,0:T(8,128)(2,1)S(1)}, bf16[512,256]{1,0:T(8,128)(2,1)S(1)}) all-reduce(f32[512,256]{1,0:T(8,128)S(1)} %fusion.34, f32[512,256]{1,0:T(8,128)S(1)} %fusion.36), channel_id=1, replica_groups=mesh['row'=16,'col'=16] {'col'}, use_global_device_ids=true, to_apply=%region_1.0 | all-reduce | flops 262144 | bytes 1572864 | tf_op jit(solution)/shard_map/psum | solution.py:34
  131.6 0.0 all-gather.5.cloned.1.call-done
  131.6 4.5 %fusion.11 = bf16[8,128,512]{2,0,1:T(8,128)(2,1)S(1)} fusion(bf16[32,128,512]{2,1,0:T(8,128)(2,1)} %all-gather.5.cloned.1.call-done, s32[32]{0:T(128)S(1)} %get-tuple-element.12, s32[8]{0:T(128)S(1)} %fusion.68), kind=kOutput, calls=%fused_computation.13 | convolution fusion | flops 34078976 | bytes 5243040 | tf_op jit(solution)/shard_map/ka,axp->kxp/dot_general | solution.py:40
  136.2 1.7 %convolution_bitcast_fusion = f32[8,1,128,256]{3,2,0,1:T(8,128)} fusion(bf16[8,128,512]{2,0,1:T(8,128)(2,1)S(1)} %fusion.11, bf16[512,256]{1,0:T(8,128)(2,1)S(1)} %get-tuple-element.6), kind=kOutput, calls=%fused_computation.14 | convolution fusion | flops 268435456 | bytes 2359296 | tf_op jit(solution)/shard_map/kxp,pn->kxn/dot_general | solution.py:47
  137.9 4.7 %fusion.8 = bf16[8,128,512]{2,0,1:T(8,128)(2,1)S(1)} fusion(bf16[32,128,512]{2,1,0:T(8,128)(2,1)} %all-gather.3.cloned.1.call-done, s32[32]{0:T(128)S(1)} %get-tuple-element.13, s32[8]{0:T(128)S(1)} %fusion.68), kind=kOutput, calls=%fused_computation.12 | convolution fusion | flops 34078976 | bytes 5243040 | tf_op jit(solution)/shard_map/ka,axp->kxp/dot_general | solution.py:40
  142.6 2.4 %fusion.4 = bf16[8,128,512]{2,0,1:T(8,128)(2,1)S(1)} fusion(bf16[32,128,512]{2,1,0:T(8,128)(2,1)S(1)} %copy-done.1, s32[32]{0:T(128)S(1)} %get-tuple-element.13, s32[8]{0:T(128)S(1)} %fusion.69), kind=kOutput, calls=%fused_computation.6 | convolution fusion | flops 33554688 | bytes 5243040 | tf_op jit(solution)/shard_map/ia,axp->ixp/dot_general | solution.py:37
  145.0 1.6 fusion.18
  146.6 0.5 copy-done
  147.2 2.4 %fusion = bf16[8,128,512]{2,0,1:T(8,128)(2,1)S(1)} fusion(bf16[32,128,512]{2,1,0:T(8,128)(2,1)S(1)} %copy-done, s32[32]{0:T(128)S(1)} %get-tuple-element.12, s32[8]{0:T(128)S(1)} %fusion.69), kind=kOutput, calls=%fused_computation.2 | convolution fusion | flops 33554688 | bytes 5243040 | tf_op jit(solution)/shard_map/ia,axp->ixp/dot_general | solution.py:37
  149.5 2.4 %bitcast_subtract_fusion = f32[8,1,128,8,1,128]{5,2,3,0,4,1:T(8,128)S(1)} fusion(f32[8,128,8,128]{3,1,2,0:T(8,128)S(1)} %fusion.18, f32[8,1,128,8,1,128]{5,4,3,2,1,0:T(1,128)S(1)} %copy-done.2, bf16[8,128,512]{2,0,1:T(8,128)(2,1)S(1)} %fusion, bf16[8,128,512]{2,0,1:T(8,128)(2,1)S(1)} %fusion.11), kind=kOutput, calls=%fused_computation | convolution fusion | flops 1075838976 | bytes 14680064 | tf_op jit(solution)/shard_map/ixp,kyp->ixky/dot_general | solution.py:43
  151.9 6.3 %copy.26 = f32[8,1,128,8,1,128]{5,4,3,2,1,0:T(1,128)} copy(f32[8,1,128,8,1,128]{5,2,3,0,4,1:T(8,128)S(1)} %bitcast_subtract_fusion) | data formatting | bytes 8388608
  158.2 2.9 %fusion.16 = f32[8,1,128,256]{3,2,1,0:T(8,128)} fusion(f32[8,1,128,256]{3,2,0,1:T(8,128)S(1)} %copy-done.3, f32[8,1,128,256]{3,2,1,0:T(8,128)} %param.11, bf16[8,128,512]{2,0,1:T(8,128)(2,1)S(1)} %fusion.8, bf16[512,256]{1,0:T(8,128)(2,1)S(1)} %get-tuple-element.7), kind=kOutput, calls=%fused_computation.18 | convolution fusion | flops 268959744 | bytes 4456448 | tf_op jit(solution)/shard_map/kxp,pn->kxn/dot_general | solution.py:47
  (15 shorter events, 0.0 us)
Async XLA Ops:
  7.2 54.3 %copy-start.4 = (bf16[2,32,256]{2,1,0:T(8,128)(2,1)S(1)}, bf16[2,32,256]{2,1,0:T(8,128)(2,1)}, u32[]{:S(2)}) copy-start(bf16[2,32,256]{2,1,0:T(8,128)(2,1)} %param.9) | copy-start | bytes 98308
  7.2 54.9 %copy-start.5 = (s32[2,32]{1,0:T(2,128)S(1)}, s32[2,32]{1,0:T(2,128)}, u32[]{:S(2)}) copy-start(s32[2,32]{1,0:T(2,128)} %param.10) | copy-start | bytes 772
  7.2 124.4 %all-gather.5.cloned.1.call-start = ((), (), s32[]{:S(2)}) async-start(), calls=%async_computation.1 | async-start | bytes 4456448 | tf_op jit(solution)/shard_map/all_gather | solution.py:31
  33.8 104.1 %all-gather.3.cloned.1.call-start = ((), (), s32[]{:S(2)}) async-start(), calls=%async_computation | async-start | bytes 4456448 | tf_op jit(solution)/shard_map/all_gather | solution.py:31
  137.9 4.7 %copy-start.1 = (bf16[32,128,512]{2,1,0:T(8,128)(2,1)S(1)}, bf16[32,128,512]{2,1,0:T(8,128)(2,1)}, u32[]{:S(2)}) copy-start(bf16[32,128,512]{2,1,0:T(8,128)(2,1)} %all-gather.3.cloned.1.call-done) | copy-start | bytes 12582916
  145.0 2.2 %copy-start = (bf16[32,128,512]{2,1,0:T(8,128)(2,1)S(1)}, bf16[32,128,512]{2,1,0:T(8,128)(2,1)}, u32[]{:S(2)}) copy-start(bf16[32,128,512]{2,1,0:T(8,128)(2,1)} %all-gather.5.cloned.1.call-done) | copy-start | bytes 12582916
  147.2 2.4 %copy-start.2 = (f32[8,1,128,8,1,128]{5,4,3,2,1,0:T(1,128)S(1)}, f32[8,1,128,8,1,128]{5,4,3,2,1,0:T(1,128)}, u32[]{:S(2)}) copy-start(f32[8,1,128,8,1,128]{5,4,3,2,1,0:T(1,128)} %param.6) | copy-start | bytes 12582916
  151.9 6.3 %copy-start.3 = (f32[8,1,128,256]{3,2,0,1:T(8,128)S(1)}, f32[8,1,128,256]{3,2,0,1:T(8,128)}, u32[]{:S(2)}) copy-start(f32[8,1,128,256]{3,2,0,1:T(8,128)} %convolution_bitcast_fusion) | copy-start | bytes 3145732
Sparse Core Ops, SparseCore 0:
  33.9 43.4 all-gather.4
  79.3 43.1 all-gather.2
where the time goes:
time: 168 us
  blocking collectives  119 us (71%)
  matrix products  25.8 us (15%)
  between operations  14.2 us (8%)
  local copies, waits for them, and re-layouts  9.27 us (6%)
    psum x1, blocking collectives, shards(): partial_value = lax.psum(local_term, 'col').astype(jnp.bfloat16)  69.4 us
    all_gather x2, blocking collectives, shards(): column_tiles = lax.all_gather(solved_piece, 'row', axis=1, tiled=True)  49.2 us
    dot_general x2, matrix products, shards(): jnp.einsum('ka,axp->kxp', pick_cols, all_tiles, preferred_element_type=jn...  9.25 us
    unnamed x13, local copies, waits for them, and re-layouts  6.89 us
    dot_general x2, matrix products, shards(): jnp.einsum('ia,axp->ixp', pick_rows, all_tiles, preferred_element_type=jn...  4.72 us
    dot_general x2, matrix products, shards(): jnp.einsum('kxp,pn->kxn', col_set, partial_value, preferred_element_type=...  4.65 us
    dot_general x2, matrix products, shards(): jnp.einsum('ixp,kyp->ixky', row_set, col_set, preferred_element_type=jnp....  4 us
  transfers between devices with their start and end apart: 2, of which 0 were waited for; matrix products, arithmetic and copies ran while one was open for 6% of the time, Pallas kernels for 0%

commit v1 on v0

--- a/solution.py
+++ b/solution.py
@@ -27,7 +27,10 @@
         solved_piece = jnp.einsum(
             "axq,pq->axp", own_rows, factor, preferred_element_type=jnp.float32
         ).astype(jnp.bfloat16)
-        column_tiles = lax.all_gather(solved_piece, "row", axis=1, tiled=True)
+        part_next = lax.axis_size("row")
+        s_next = jnp.stack([solved_piece] * part_next)
+        h_now = lax.all_to_all(s_next, "row", 0, 0)
+        column_tiles = jnp.concatenate(h_now, axis=1)
         all_tiles = lax.all_gather(column_tiles, "col", axis=0, tiled=True)
         columns = lax.dynamic_slice_in_dim(factor, col_index * shard_rows, shard_rows, 1)
         local_term = jnp.dot(columns, panel_rhs[which_panel], preferred_element_type=jnp.float32)

time: 168 us -> 149 us (0.89)
  blocking collectives: 119 us -> 98.9 us
    all_gather x2 -> x0, blocking collectives: 49.2 us -> none  [shards(): column_tiles = lax.all_gather(solved_piece, 'row', axis=1, tiled=True)]
    all_to_all x0 -> x2, blocking collectives: none -> 25.5 us  [shards(): h_now = lax.all_to_all(s_next, 'row', 0, 0)]
    psum x1, blocking collectives: 69.4 us -> 73.4 us  [shards(): partial_value = lax.psum(local_term, 'col').astype(jnp.bfloat16)]
    unnamed x13 -> x15, local copies, waits for them, and re-layouts: 6.89 us -> 6.89 us
where the time goes in v1:
time: 149 us
  blocking collectives  98.9 us (66%)
  matrix products  25.7 us (17%)
  between operations  14.2 us (10%)
  local copies, waits for them, and re-layouts  9.61 us (6%)
    psum x1, blocking collectives, shards(): partial_value = lax.psum(local_term, 'col').astype(jnp.bfloat16)  73.4 us
    all_to_all x2, blocking collectives, shards(): h_now = lax.all_to_all(s_next, 'row', 0, 0)  25.5 us
    dot_general x2, matrix products, shards(): jnp.einsum('ka,axp->kxp', pick_cols, all_tiles, preferred_element_type=jn...  9.25 us
    unnamed x15, local copies, waits for them, and re-layouts  6.89 us
    dot_general x2, matrix products, shards(): jnp.einsum('ia,axp->ixp', pick_rows, all_tiles, preferred_element_type=jn...  4.72 us
    dot_general x2, matrix products, shards(): jnp.einsum('kxp,pn->kxn', col_set, partial_value, preferred_element_type=...  4.64 us
    dot_general x2, matrix products, shards(): jnp.einsum('ixp,kyp->ixky', row_set, col_set, preferred_element_type=jnp....  3.96 us
  transfers between devices with their start and end apart: 2, of which 0 were waited for; matrix products, arithmetic and copies ran while one was open for 6% of the time, Pallas kernels for 0%

profile of v1, /device:TPU:0, one launch (start us, length us, event | category | flops | bytes accessed | tf_op | source)
XLA Modules:
  0.0 148.6 jit_solution(8437274021383018492)
XLA Ops:
  7.2 0.0 all-gather.5.cloned.1.call-start
  7.2 1.1 fusion.83
  8.4 1.3 convolution_convert_fusion
  9.7 13.6 %all_to_all.10 = bf16[16,2,8,512]{3,2,1,0:T(8,128)(2,1)S(1)} all-to-all(bf16[16,2,8,512]{3,2,1,0:T(8,128)(2,1)S(1)} %stack.5), channel_id=1, replica_groups=mesh['row'=16,'col'=16] {'row'}, dimensions={0} | all-to-all | bytes 524288 | tf_op jit(solution)/shard_map/all_to_all | solution.py:32
  23.3 0.7 copy.103
  24.1 0.0 all-gather.3.cloned.1.call-start
  24.1 1.3 convolution_convert_fusion.1
  25.5 11.9 %all_to_all.11 = bf16[16,2,8,512]{3,2,1,0:T(8,128)(2,1)S(1)} all-to-all(bf16[16,2,8,512]{3,2,1,0:T(8,128)(2,1)S(1)} %stack.4), channel_id=1, replica_groups=mesh['row'=16,'col'=16] {'row'}, dimensions={0} | all-to-all | bytes 524288 | tf_op jit(solution)/shard_map/all_to_all | solution.py:32
  37.4 0.7 copy.104
  38.1 0.1 fusion.82
  38.2 0.3 fusion.44
  38.5 0.3 fusion.46
  38.8 73.4 %all-reduce.2 = (bf16[512,256]{1,0:T(8,128)(2,1)S(1)}, bf16[512,256]{1,0:T(8,128)(2,1)S(1)}) all-reduce(f32[512,256]{1,0:T(8,128)S(1)} %fusion.44, f32[512,256]{1,0:T(8,128)S(1)} %fusion.46), channel_id=1, replica_groups=mesh['row'=16,'col'=16] {'col'}, use_global_device_ids=true, to_apply=%region_1.0 | all-reduce | flops 262144 | bytes 1572864 | tf_op jit(solution)/shard_map/psum | solution.py:37
  112.2 0.0 all-gather.5.cloned.1.call-done
  112.3 4.5 %fusion.17 = bf16[8,128,512]{2,0,1:T(8,128)(2,1)S(1)} fusion(bf16[32,128,512]{2,1,0:T(8,128)(2,1)} %all-gather.5.cloned.1.call-done, s32[32]{0:T(128)S(1)} %get-tuple-element.16, s32[8]{0:T(128)S(1)} %fusion.78), kind=kOutput, calls=%fused_computation.13 | convolution fusion | flops 34078976 | bytes 5243040 | tf_op jit(solution)/shard_map/ka,axp->kxp/dot_general | solution.py:43
  116.8 1.7 %convolution_bitcast_fusion = f32[8,1,128,256]{3,2,0,1:T(8,128)} fusion(bf16[8,128,512]{2,0,1:T(8,128)(2,1)S(1)} %fusion.17, bf16[512,256]{1,0:T(8,128)(2,1)S(1)} %get-tuple-element.10), kind=kOutput, calls=%fused_computation.16 | convolution fusion | flops 268435456 | bytes 2359296 | tf_op jit(solution)/shard_map/kxp,pn->kxn/dot_general | solution.py:50
  118.5 4.7 %fusion.11 = bf16[8,128,512]{2,0,1:T(8,128)(2,1)S(1)} fusion(bf16[32,128,512]{2,1,0:T(8,128)(2,1)} %all-gather.3.cloned.1.call-done, s32[32]{0:T(128)S(1)} %get-tuple-element.17, s32[8]{0:T(128)S(1)} %fusion.78), kind=kOutput, calls=%fused_computation.11 | convolution fusion | flops 34078976 | bytes 5243040 | tf_op jit(solution)/shard_map/ka,axp->kxp/dot_general | solution.py:43
  123.2 2.4 %fusion.23 = bf16[8,128,512,1]{2,0,1,3:T(8,128)(2,1)S(1)} fusion(bf16[32,128,512]{2,1,0:T(8,128)(2,1)S(1)} %copy-done.1, s32[32]{0:T(128)S(1)} %get-tuple-element.17, s32[8]{0:T(128)S(1)} %fusion.79), kind=kOutput, calls=%fused_computation.15 | convolution fusion | flops 34078976 | bytes 5243040 | tf_op jit(solution)/shard_map/ia,axp->ixp/dot_general | solution.py:40
  125.6 1.6 %fusion.31 = f32[8,128,8,128]{3,1,2,0:T(8,128)S(1)} fusion(bf16[8,128,512,1]{2,0,1,3:T(8,128)(2,1)S(1)} %fusion.23, bf16[8,128,512]{2,0,1:T(8,128)(2,1)S(1)} %fusion.11), kind=kOutput, calls=%fused_computation.25 | convolution fusion | flops 1073741824 | bytes 6291456 | tf_op jit(solution)/shard_map/ixp,kyp->ixky/dot_general | solution.py:46
  127.3 0.5 copy-done
  127.8 2.4 %fusion.20 = bf16[8,128,512,1]{2,0,1,3:T(8,128)(2,1)S(1)} fusion(bf16[32,128,512]{2,1,0:T(8,128)(2,1)S(1)} %copy-done, s32[32]{0:T(128)S(1)} %get-tuple-element.16, s32[8]{0:T(128)S(1)} %fusion.79), kind=kOutput, calls=%fused_computation.14 | convolution fusion | flops 34078976 | bytes 5243040 | tf_op jit(solution)/shard_map/ia,axp->ixp/dot_general | solution.py:40
  130.2 2.3 %bitcast_subtract_fusion = f32[8,1,128,8,1,128]{5,2,3,0,4,1:T(8,128)S(1)} fusion(f32[8,128,8,128]{3,1,2,0:T(8,128)S(1)} %fusion.31, f32[8,1,128,8,1,128]{5,4,3,2,1,0:T(1,128)S(1)} %copy-done.2, bf16[8,128,512,1]{2,0,1,3:T(8,128)(2,1)S(1)} %fusion.20, bf16[8,128,512]{2,0,1:T(8,128)(2,1)S(1)} %fusion.17), kind=kOutput, calls=%fused_computation | convolution fusion | flops 1075838976 | bytes 14680064 | tf_op jit(solution)/shard_map/ixp,kyp->ixky/dot_general | solution.py:46
  132.5 6.3 %copy.56 = f32[8,1,128,8,1,128]{5,4,3,2,1,0:T(1,128)} copy(f32[8,1,128,8,1,128]{5,2,3,0,4,1:T(8,128)S(1)} %bitcast_subtract_fusion) | data formatting | bytes 8388608
  138.8 2.9 %fusion.28 = f32[8,1,128,256]{3,2,1,0:T(8,128)} fusion(f32[8,1,128,256]{3,2,0,1:T(8,128)S(1)} %copy-done.4, f32[8,1,128,256]{3,2,1,0:T(8,128)} %param.11, bf16[8,128,512]{2,0,1:T(8,128)(2,1)S(1)} %fusion.11, bf16[512,256]{1,0:T(8,128)(2,1)S(1)} %get-tuple-element.11), kind=kOutput, calls=%fused_computation.20 | convolution fusion | flops 268959744 | bytes 4456448 | tf_op jit(solution)/shard_map/kxp,pn->kxn/dot_general | solution.py:50
  (21 shorter events, 0.1 us)
Async XLA Ops:
  7.2 30.9 %copy-start.3 = (bf16[2,512,512]{2,1,0:T(8,128)(2,1)S(1)}, bf16[2,512,512]{2,1,0:T(8,128)(2,1)}, u32[]{:S(2)}) copy-start(bf16[2,512,512]{2,1,0:T(8,128)(2,1)} %param.8) | copy-start | bytes 3145732
  7.2 31.0 %copy-start.5 = (bf16[2,32,256]{2,1,0:T(8,128)(2,1)S(1)}, bf16[2,32,256]{2,1,0:T(8,128)(2,1)}, u32[]{:S(2)}) copy-start(bf16[2,32,256]{2,1,0:T(8,128)(2,1)} %param.9) | copy-start | bytes 98308
  7.2 105.1 %all-gather.5.cloned.1.call-start = ((), (), s32[]{:S(2)}) async-start(), calls=%async_computation.3 | async-start | bytes 4456448 | tf_op jit(solution)/shard_map/all_gather | solution.py:34
  7.2 31.6 %copy-start.6 = (s32[2,32]{1,0:T(2,128)S(1)}, s32[2,32]{1,0:T(2,128)}, u32[]{:S(2)}) copy-start(s32[2,32]{1,0:T(2,128)} %param.10) | copy-start | bytes 772
  24.1 94.4 %all-gather.3.cloned.1.call-start = ((), (), s32[]{:S(2)}) async-start(), calls=%async_computation.2 | async-start | bytes 4456448 | tf_op jit(solution)/shard_map/all_gather | solution.py:34
  118.5 4.7 %copy-start.1 = (bf16[32,128,512]{2,1,0:T(8,128)(2,1)S(1)}, bf16[32,128,512]{2,1,0:T(8,128)(2,1)}, u32[]{:S(2)}) copy-start(bf16[32,128,512]{2,1,0:T(8,128)(2,1)} %all-gather.3.cloned.1.call-done) | copy-start | bytes 12582916
  125.6 2.2 %copy-start = (bf16[32,128,512]{2,1,0:T(8,128)(2,1)S(1)}, bf16[32,128,512]{2,1,0:T(8,128)(2,1)}, u32[]{:S(2)}) copy-start(bf16[32,128,512]{2,1,0:T(8,128)(2,1)} %all-gather.5.cloned.1.call-done) | copy-start | bytes 12582916
  127.8 2.4 %copy-start.2 = (f32[8,1,128,8,1,128]{5,4,3,2,1,0:T(1,128)S(1)}, f32[8,1,128,8,1,128]{5,4,3,2,1,0:T(1,128)}, u32[]{:S(2)}) copy-start(f32[8,1,128,8,1,128]{5,4,3,2,1,0:T(1,128)} %param.6) | copy-start | bytes 12582916
  132.5 6.3 %copy-start.4 = (f32[8,1,128,256]{3,2,0,1:T(8,128)S(1)}, f32[8,1,128,256]{3,2,0,1:T(8,128)}, u32[]{:S(2)}) copy-start(f32[8,1,128,256]{3,2,0,1:T(8,128)} %convolution_bitcast_fusion) | copy-start | bytes 3145732
Sparse Core Ops, SparseCore 0:
  24.2 42.7 all-gather.4
  69.4 42.9 all-gather.2
